TPU v7x, 32 devices: a whole 2x2x4 slice. The times are simulated.
32 devices in a mesh: row: 2 (over core), col: 4 (over z), ind: 4 (over y, x).
Axes of the slice: x: 2, y: 2, z: 4, core: 2. Of those that a mesh axis runs over, the one named last changes fastest.
Arguments:
- dosages: bfloat16 [4096, 1024], P('ind', ('row', 'col'))
- annotations: bfloat16 [1024, 1024], P('ind', ('row', 'col')), may hold values from -6 to 6
- window_end: int32 [1024], P(('row', 'col')), may hold values from 512 to 1024, as said below
Outputs:
- ld_scores: float32 [1024, 1024], P('ind', ('row', 'col'))
Inputs may be any that keep to these rules, and one draw needn't show every extreme that they name: window_end is nondecreasing, window_end[j] > j, and window_end[j] <= min(1024, (j // 128 + 4) * 128), the last bound reached in every draw.
All inputs are finite; a program needn't handle non-finite values.
Results may differ from a plain program's by a relative error of at most 0.0029.
Values may be sent and summed in bfloat16 or wider, within the bound.
A program may use at most 64 MiB of HBM per device.

v0:
```python
import jax
import jax.numpy as jnp
from jax import lax
from jax.sharding import PartitionSpec as P


def from_behind(array, axis, by):
    count = lax.axis_size(axis)
    pairs = [(i, i + by) for i in range(count) if 0 <= i + by < count]
    return lax.ppermute(array, axis, pairs)


def per_device(dosages, annotations, window_end):
    band_count = lax.axis_size("col")
    column_index = lax.axis_index("col")
    tile_size = dosages.shape[1]
    ind_rows = dosages.shape[0]
    ann_rows = annotations.shape[0]
    group_width = band_count * tile_size
    sample_count = ind_rows * lax.axis_size("ind")
    window_ends = lax.all_gather(window_end, "col", axis=0, tiled=True)
    group_x, group_a = (
        lax.all_gather(dosages, "col", axis=1, tiled=True),
        lax.all_gather(annotations, "col", axis=1, tiled=True),
    )
    next_x, next_a = from_behind((group_x, group_a), "row", -1)
    wide_x = jnp.concatenate([group_x, next_x], axis=1)
    wide_a = jnp.concatenate([group_a, next_a], axis=1)
    band_x = lax.dynamic_slice_in_dim(wide_x, column_index * tile_size, group_width, 1)
    band_a = lax.dynamic_slice_in_dim(wide_a, column_index * tile_size, group_width, 1)
    rows_x = group_x.reshape(ind_rows, band_count, tile_size)
    cols_x = band_x.reshape(ind_rows, band_count, tile_size)
    partial_gram = jnp.einsum("inb,ine->nbe", rows_x, cols_x, preferred_element_type=jnp.float32)
    gram = lax.psum(partial_gram, "ind")
    correlation_matrix = gram / sample_count
    raw_rsquared = correlation_matrix * correlation_matrix
    unbiased_rsquared = raw_rsquared - (1.0 - raw_rsquared) / (sample_count - 2)
    group_start = lax.axis_index("row") * group_width
    block_ids = jnp.arange(band_count, dtype=jnp.int32)[:, None, None]
    within_window = jnp.arange(tile_size, dtype=jnp.int32)
    row_pos = group_start + block_ids * tile_size + within_window[None, :, None]
    col_pos = group_start + (block_ids + column_index) * tile_size + within_window[None, None, :]
    limit = window_ends.reshape(band_count, tile_size)[:, :, None]
    inside = col_pos < limit
    upper = jnp.where((col_pos >= row_pos) & inside, unbiased_rsquared, 0.0).astype(jnp.bfloat16)
    strict = jnp.where((col_pos > row_pos) & inside, unbiased_rsquared, 0.0).astype(jnp.bfloat16)
    annotation_rows = group_a.reshape(ann_rows, band_count, tile_size)
    cols_a = band_a.reshape(ann_rows, band_count, tile_size)
    direct = jnp.einsum("cne,nae->cna", cols_a, upper, preferred_element_type=jnp.float32)
    mirror = jnp.einsum("cna,nae->cne", annotation_rows, strict, preferred_element_type=jnp.float32)
    direct = direct.reshape(ann_rows, group_width)
    mirror = mirror.reshape(ann_rows, group_width)
    window_acc = jnp.zeros((ann_rows, 2 * group_width), jnp.float32)
    window_acc = lax.dynamic_update_slice_in_dim(window_acc, mirror, column_index * tile_size, 1)
    window_acc = window_acc.at[:, :group_width].add(direct)
    incoming = from_behind(window_acc[:, group_width:], "row", 1)
    combined = window_acc[:, :group_width] + incoming
    ld_scores = lax.psum_scatter(combined, "col", scatter_dimension=1, tiled=True)
    return ld_scores


def solution(mesh):
    in_specs = (P("ind", ("row", "col")), P("ind", ("row", "col")), P(("row", "col")))
    out_specs = P("ind", ("row", "col"))
    return jax.shard_map(
        per_device, mesh=mesh, in_specs=in_specs, out_specs=out_specs, check_vma=False
    )
```

profile of v0, /device:TPU:0, one launch (start us, length us, event | category | flops | bytes accessed | tf_op | source)
XLA Modules:
  0.0 139.3 jit_solution(7500563988074717324)
XLA Ops:
  6.5 0.0 all-gather.3.cloned.1.call-start
  6.5 1.8 %copy.16 = bf16[1024,128]{0,1:T(8,128)(2,1)} copy(bf16[1024,128]{1,0:T(8,128)(2,1)} %param.5) | data formatting | bytes 524288 | tf_op args[0]
  8.3 0.0 all-gather.3.cloned.1.call-update
  8.4 0.0 all-reduce.2.cloned.1.call-start
  8.4 31.2 %all-gather.3.cloned.1.call-done = bf16[1024,512]{0,1:T(8,128)(2,1)} async-done(((bf16[1024,128]{0,1:T(8,128)(2,1)}), bf16[1024,512]{0,1:T(8,128)(2,1)}) %all-gather.3.cloned.1.call-update) | async-done | bytes 1048592 | tf_op jit(solution)/shard_map/all_gather | solution.py:23
  39.6 1.3 collective-permute-start
  40.9 0.9 copy.18
  41.9 14.4 %all_gather.11 = bf16[256,512]{0,1:T(8,128)(2,1)S(1)} all-gather(bf16[256,128]{0,1:T(8,128)(2,1)S(1)} %copy.18), channel_id=1, replica_groups=mesh['row'=2,'col'=4,'ind'=4] {'col'}, dimensions={1}, use_global_device_ids=true | all-gather | bytes 327680 | tf_op jit(solution)/shard_map/all_gather | solution.py:24
  56.2 1.3 collective-permute-start.1
  57.6 0.0 copy-start
  57.6 0.0 collective-permute-done
  57.6 2.3 %fusion = bf16[1024,512]{0,1:T(8,128)(2,1)S(1)} fusion(s32[]{:T(128)S(6)} %select_n.12, bf16[1024,512]{0,1:T(8,128)(2,1)} %all-gather.3.cloned.1.call-done, bf16[1024,512]{0,1:T(8,128)(2,1)S(1)} %collective-permute-done), kind=kLoop, calls=%fused_computation.3 | loop fusion | flops 2097152 | bytes 3145732 | tf_op jit(solution)/shard_map/concatenate | solution.py:27
  59.9 0.0 copy-done
  59.9 0.0 copy-start.2
  59.9 1.1 convolution_bitcast_fusion
  61.0 0.0 all-reduce.2.cloned.1.call-update
  61.1 0.0 reduce-scatter.2.cloned.1.call-start
  61.1 0.1 iota_add_fusion
  61.2 0.0 copy-done.2
  61.2 9.1 %all-gather = s32[4,1,128]{2,1,0:T(1,128)S(1)} all-gather(s32[1,1,128]{2,1,0:T(1,128)S(1)} %bitcast.26), channel_id=1, replica_groups=mesh['row'=2,'col'=4,'ind'=4] {'col'}, dimensions={0}, use_global_device_ids=true | all-gather | bytes 2560 | tf_op jit(solution)/shard_map/all_gather | solution.py:21
  70.3 0.1 iota_add_fusion.1
  70.3 33.8 %all-reduce.2.cloned.1.call-done = f32[4,128,128]{1,2,0:T(8,128)} async-done(((f32[4,128,128]{1,2,0:T(8,128)}), f32[4,128,128]{1,2,0:T(8,128)}) %all-reduce.2.cloned.1.call-update) | async-done | bytes 262160 | tf_op jit(solution)/shard_map/psum | solution.py:34
  104.2 1.2 fusion.3
  105.4 0.2 copy.20
  105.6 0.1 broadcast_in_dim.11
  105.7 0.1 constant_dynamic-update-slice_fusion
  105.8 0.0 copy-start.1
  105.8 1.5 %collective-permute-start.2 = (f32[256,512]{1,0:T(8,128)S(1)}, f32[256,512]{1,0:T(8,128)S(1)}, u32[]{:S(2)}, u32[]{:S(2)}) collective-permute-start(f32[256,512]{1,0:T(8,128)S(1)} %slice.29), channel_id=1, source_target_pairs={{0,16},{1,17},{2,18},{3,19},{4,20},{5,21},{6,22},{7,23},{8,24},{9,... | collective-permute-start | bytes 1572872 | tf_op jit(solution)/shard_map/ppermute | solution.py:10
  107.3 0.6 compare_reduce_fusion
  107.9 0.0 collective-permute-done.1
  107.9 0.6 fusion.2
  108.6 0.0 copy-done.1
  108.6 0.4 fusion.4
  108.9 0.2 copy.23
  109.1 0.0 collective-permute-done.2
  109.1 1.6 %fusion.1 = f32[256,512]{1,0:T(8,128)} fusion(f32[256,512]{1,0:T(8,128)S(1)} %collective-permute-done.2, f32[256,512]{1,0:T(8,128)S(1)} %copy.23, f32[256,1024]{1,0:T(8,128)S(1)} %constant_dynamic-update-slice_fusion, pred[]{:T(512)} %compare_reduce_fusion), kind=kLoop, calls=%fused_computation.5 | loop fusion | flops 393216 | bytes 2097153 | tf_op jit(solution)/shard_map/add | solution.py:57
  110.7 0.0 reduce-scatter.2.cloned.1.call-update
  110.8 22.0 %reduce-scatter.2.cloned.1.call-done = f32[256,128]{1,0:T(8,128)} async-done(((f32[256,512]{1,0:T(8,128)}), f32[256,128]{1,0:T(8,128)}) %reduce-scatter.2.cloned.1.call-update) | async-done | bytes 131088 | tf_op jit(solution)/shard_map/reduce_scatter | solution.py:58
  (2 shorter events, 0.0 us)
Async XLA Ops:
  6.5 33.1 %all-gather.3.cloned.1.call-start = ((), (), s32[]{:S(2)}) async-start(), calls=%async_computation.1 | async-start | bytes 1310720 | tf_op jit(solution)/shard_map/all_gather | solution.py:23
  8.4 95.8 %all-reduce.2.cloned.1.call-start = ((), (), s32[]{:S(2)}) async-start(), calls=%async_computation.2 | async-start | bytes 524288 | tf_op jit(solution)/shard_map/psum | solution.py:34
  39.6 17.9 %collective-permute-start = (bf16[1024,512]{0,1:T(8,128)(2,1)}, bf16[1024,512]{0,1:T(8,128)(2,1)S(1)}, u32[]{:S(2)}, u32[]{:S(2)}) collective-permute-start(bf16[1024,512]{0,1:T(8,128)(2,1)} %all-gather.3.cloned.1.call-done), channel_id=1, source_target_pairs={{16,0},{17,1},{18,2},{19,3},{20,4},{21,5},{22,6},{23,7},{24,8},{25... | collective-permute-start | bytes 3145736 | tf_op jit(solution)/shard_map/ppermute | solution.py:10
  56.2 51.7 %collective-permute-start.1 = (bf16[256,512]{0,1:T(8,128)(2,1)S(1)}, bf16[256,512]{0,1:T(8,128)(2,1)S(1)}, u32[]{:S(2)}, u32[]{:S(2)}) collective-permute-start(bf16[256,512]{0,1:T(8,128)(2,1)S(1)} %all_gather.11), channel_id=1, source_target_pairs={{16,0},{17,1},{18,2},{19,3},{20,4},{21,5},{22,6},{23,7},{24,8},{25... | collective-permute-start | bytes 786440 | tf_op jit(solution)/shard_map/ppermute | solution.py:10
  57.6 2.3 %copy-start = (bf16[1024,512]{0,1:T(8,128)(2,1)S(1)}, bf16[1024,512]{0,1:T(8,128)(2,1)}, u32[]{:S(2)}) copy-start(bf16[1024,512]{0,1:T(8,128)(2,1)} %all-gather.3.cloned.1.call-done) | copy-start | bytes 3145732
  59.9 1.3 copy-start.2
  61.1 71.7 %reduce-scatter.2.cloned.1.call-start = ((), (), s32[]{:S(2)}) async-start(), calls=%async_computation.3 | async-start | bytes 655360 | tf_op jit(solution)/shard_map/reduce_scatter | solution.py:58
  105.8 2.8 %copy-start.1 = (f32[4,128,128]{1,2,0:T(8,128)S(1)}, f32[4,128,128]{1,2,0:T(8,128)}, u32[]{:S(2)}) copy-start(f32[4,128,128]{1,2,0:T(8,128)} %all-reduce.2.cloned.1.call-done) | copy-start | bytes 786436
  105.8 3.3 %collective-permute-start.2 = (f32[256,512]{1,0:T(8,128)S(1)}, f32[256,512]{1,0:T(8,128)S(1)}, u32[]{:S(2)}, u32[]{:S(2)}) collective-permute-start(f32[256,512]{1,0:T(8,128)S(1)} %slice.29), channel_id=1, source_target_pairs={{0,16},{1,17},{2,18},{3,19},{4,20},{5,21},{6,22},{7,23},{8,24},{9,... | collective-permute-start | bytes 1572872 | tf_op jit(solution)/shard_map/ppermute | solution.py:10
Sparse Core Ops, SparseCore 0:
  8.9 30.6 all-gather.2
  61.2 42.9 all-reduce.1
  110.9 21.8 reduce-scatter.1
where the time goes:
time: 140 us; the launch traced here: 139 us
  waiting for transfers between devices  87.1 us (62%)
  blocking collectives  23.5 us (17%)
  between operations  13.3 us (10%)
  other arithmetic  5.3 us (4%)
  starting transfers between devices  4.1 us (3%)
  local copies, waits for them, and re-layouts  3.35 us (2%)
  matrix products  2.71 us (2%)
    psum x1, waiting for transfers between devices, per_device(): gram = lax.psum(partial_gram, 'ind')  33.8 us
    all_gather x1, waiting for transfers between devices, per_device(): lax.all_gather(dosages, 'col', axis=1, tiled=True)  31.2 us
    reduce_scatter x1, waiting for transfers between devices, per_device(): lax.psum_scatter(combined, 'col', scatter_dimension=1, tiled=True)  22 us
    all_gather x1, blocking collectives, per_device(): lax.all_gather(annotations, 'col', axis=1, tiled=True)  14.4 us
    all_gather x1, blocking collectives, per_device(): window_ends = lax.all_gather(window_end, 'col', axis=0, tiled=True)  9.09 us
    ppermute x3, starting transfers between devices, from_behind(): return lax.ppermute(array, axis, pairs)  4.02 us
  transfers between devices with their start and end apart: 6, of which 3 were waited for; matrix products, arithmetic and copies ran while one was open for 6% of the time, Pallas kernels for 0%

commit v1 on v0

--- a/solution.py
+++ b/solution.py
@@ -2,6 +2,12 @@
 import jax.numpy as jnp
 from jax import lax
 from jax.sharding import PartitionSpec as P
+
+
+def summed_here(x, axis):
+    parts = lax.all_gather(x, axis, axis=0, tiled=False)
+    acc = parts.sum(axis=0)
+    return acc
 
 
 def from_behind(array, axis, by):
@@ -31,7 +37,7 @@
     rows_x = group_x.reshape(ind_rows, band_count, tile_size)
     cols_x = band_x.reshape(ind_rows, band_count, tile_size)
     partial_gram = jnp.einsum("inb,ine->nbe", rows_x, cols_x, preferred_element_type=jnp.float32)
-    gram = lax.psum(partial_gram, "ind")
+    gram = summed_here(partial_gram, "ind")
     correlation_matrix = gram / sample_count
     raw_rsquared = correlation_matrix * correlation_matrix
     unbiased_rsquared = raw_rsquared - (1.0 - raw_rsquared) / (sample_count - 2)

time: 140 us -> 110 us (0.79)
  waiting for transfers between devices: 87.1 us -> 57.9 us
  matrix products: 2.71 us -> 1.06 us
    psum x1 -> x0, waiting for transfers between devices: 33.8 us -> none  [per_device(): gram = lax.psum(partial_gram, 'ind')]
    ppermute x3, waiting for transfers between devices: 0.01 us -> 3.45 us  [from_behind(): return lax.ppermute(array, axis, pairs)]
  transfers between devices with their start and end apart: 6 -> 6, of which waited for: 3 -> 4; matrix products, arithmetic and copies ran while one was open for 6% -> 4% of each run, Pallas kernels for 0% -> 0%
where the time goes in v1:
time: 110 us
  waiting for transfers between devices  57.9 us (53%)
  blocking collectives  23 us (21%)
  between operations  13.3 us (12%)
  other arithmetic  6.51 us (6%)
  starting transfers between devices  4.25 us (4%)
  local copies, waits for them, and re-layouts  3.48 us (3%)
    all_gather x1, waiting for transfers between devices, per_device(): lax.all_gather(dosages, 'col', axis=1, tiled=True)  31.2 us
    reduce_scatter x1, waiting for transfers between devices, per_device(): lax.psum_scatter(combined, 'col', scatter_dimension=1, tiled=True)  22 us
    all_gather x1, blocking collectives, per_device(): lax.all_gather(annotations, 'col', axis=1, tiled=True)  13.9 us
    all_gather x1, blocking collectives, per_device(): window_ends = lax.all_gather(window_end, 'col', axis=0, tiled=True)  9.16 us
    ppermute x3, starting transfers between devices, from_behind(): return lax.ppermute(array, axis, pairs)  4.17 us
    ppermute x3, waiting for transfers between devices, from_behind(): return lax.ppermute(array, axis, pairs)  3.45 us
    concatenate x1, other arithmetic, per_device(): wide_x = jnp.concatenate([group_x, next_x], axis=1)  2.21 us
  transfers between devices with their start and end apart: 6, of which 4 were waited for; matrix products, arithmetic and copies ran while one was open for 4% of the time, Pallas kernels for 0%

profile of v1, /device:TPU:0, one launch (start us, length us, event | category | flops | bytes accessed | tf_op | source)
XLA Modules:
  0.0 109.5 jit_solution(13344527033893841829)
XLA Ops:
  6.5 0.0 all-gather.5.cloned.1.call-start
  6.5 1.8 %copy.16 = bf16[1024,128]{0,1:T(8,128)(2,1)} copy(bf16[1024,128]{1,0:T(8,128)(2,1)} %param.5) | data formatting | bytes 524288 | tf_op args[0]
  8.3 0.0 all-gather.5.cloned.1.call-update
  8.4 0.0 all-gather.7.cloned.1.call-start
  8.4 31.2 %all-gather.5.cloned.1.call-done = bf16[1024,512]{0,1:T(8,128)(2,1)} async-done(((bf16[1024,128]{0,1:T(8,128)(2,1)}), bf16[1024,512]{0,1:T(8,128)(2,1)}) %all-gather.5.cloned.1.call-update) | async-done | bytes 1048592 | tf_op jit(solution)/shard_map/all_gather | solution.py:29
  39.6 1.3 %collective-permute-start = (bf16[1024,512]{0,1:T(8,128)(2,1)}, bf16[1024,512]{0,1:T(8,128)(2,1)S(1)}, u32[]{:S(2)}, u32[]{:S(2)}) collective-permute-start(bf16[1024,512]{0,1:T(8,128)(2,1)} %all-gather.5.cloned.1.call-done), channel_id=1, source_target_pairs={{16,0},{17,1},{18,2},{19,3},{20,4},{21,5},{22,6},{23,7},{24,8},{25... | collective-permute-start | bytes 3145736 | tf_op jit(solution)/shard_map/ppermute | solution.py:16
  40.9 0.0 copy-start
  40.9 3.4 %collective-permute-done = bf16[1024,512]{0,1:T(8,128)(2,1)S(1)} collective-permute-done((bf16[1024,512]{0,1:T(8,128)(2,1)}, bf16[1024,512]{0,1:T(8,128)(2,1)S(1)}, u32[]{:S(2)}, u32[]{:S(2)}) %collective-permute-start) | collective-permute-done | bytes 1048608 | tf_op jit(solution)/shard_map/ppermute | solution.py:16
  44.4 2.2 %fusion = bf16[1024,512]{0,1:T(8,128)(2,1)S(1)} fusion(s32[]{:T(128)S(6)} %select_n.12, bf16[1024,512]{0,1:T(8,128)(2,1)} %all-gather.5.cloned.1.call-done, bf16[1024,512]{0,1:T(8,128)(2,1)S(1)} %collective-permute-done), kind=kLoop, calls=%fused_computation.3 | loop fusion | flops 2097152 | bytes 3145732 | tf_op jit(solution)/shard_map/concatenate | solution.py:33
  46.6 0.0 copy-done
  46.6 0.0 copy-start.1
  46.6 0.4 convolution_bitcast_fusion
  47.1 0.0 copy-start.2
  47.1 0.8 copy.18
  47.9 0.0 all-gather.7.cloned.1.call-update
  47.9 0.0 reduce-scatter.2.cloned.1.call-start
  48.0 0.0 copy-done.1
  48.0 0.1 copy.20
  48.1 13.9 %all_gather.19 = bf16[256,512]{0,1:T(8,128)(2,1)S(1)} all-gather(bf16[256,128]{0,1:T(8,128)(2,1)S(1)} %copy.20), channel_id=1, replica_groups=mesh['row'=2,'col'=4,'ind'=4] {'col'}, dimensions={1}, use_global_device_ids=true | all-gather | bytes 327680 | tf_op jit(solution)/shard_map/all_gather | solution.py:30
  62.0 1.3 %collective-permute-start.1 = (bf16[256,512]{0,1:T(8,128)(2,1)S(1)}, bf16[256,512]{0,1:T(8,128)(2,1)S(1)}, u32[]{:S(2)}, u32[]{:S(2)}) collective-permute-start(bf16[256,512]{0,1:T(8,128)(2,1)S(1)} %all_gather.19), channel_id=1, source_target_pairs={{16,0},{17,1},{18,2},{19,3},{20,4},{21,5},{22,6},{23,7},{24,8},{25... | collective-permute-start | bytes 786440 | tf_op jit(solution)/shard_map/ppermute | solution.py:16
  63.3 0.0 copy-done.2
  63.3 9.2 %all-gather.1 = s32[4,1,128]{2,1,0:T(1,128)S(1)} all-gather(s32[1,1,128]{2,1,0:T(1,128)S(1)} %bitcast.28), channel_id=1, replica_groups=mesh['row'=2,'col'=4,'ind'=4] {'col'}, dimensions={0}, use_global_device_ids=true | all-gather | bytes 2560 | tf_op jit(solution)/shard_map/all_gather | solution.py:27
  72.4 0.1 iota_add_fusion
  72.5 0.1 iota_add_fusion.1
  72.6 1.2 %all-gather.7.cloned.1.call-done = f32[16,128,128]{2,1,0:T(8,128)} async-done(((f32[4,128,128]{2,1,0:T(8,128)}), f32[16,128,128]{2,1,0:T(8,128)}) %all-gather.7.cloned.1.call-update) | async-done | bytes 1048592 | tf_op jit(solution)/shard_map/all_gather | solution.py:8
  73.8 1.3 %reduce_sum.9 = f32[4,128,128]{2,1,0:T(8,128)S(1)} reduce(f32[4,4,128,128]{3,2,1,0:T(8,128)} %bitcast.24, f32[]{:T(128)} %constant.49.clone.1), dimensions={0}, to_apply=%region_1.2 | reduce | flops 196608 | bytes 1310724 | tf_op jit(solution)/shard_map/reduce_sum | solution.py:9
  75.1 0.1 copy.30
  75.2 0.3 fusion.3
  75.5 0.2 copy.22
  75.7 0.1 broadcast_in_dim.11
  75.8 0.1 constant_dynamic-update-slice_fusion
  75.9 1.6 %collective-permute-start.2 = (f32[256,512]{1,0:T(8,128)S(1)}, f32[256,512]{1,0:T(8,128)S(1)}, u32[]{:S(2)}, u32[]{:S(2)}) collective-permute-start(f32[256,512]{1,0:T(8,128)S(1)} %slice.29), channel_id=1, source_target_pairs={{0,16},{1,17},{2,18},{3,19},{4,20},{5,21},{6,22},{7,23},{8,24},{9,... | collective-permute-start | bytes 1572872 | tf_op jit(solution)/shard_map/ppermute | solution.py:16
  77.5 0.6 compare_reduce_fusion
  78.2 0.0 collective-permute-done.1
  78.2 0.6 fusion.2
  78.8 0.4 fusion.4
  79.2 0.2 copy.25
  79.4 0.0 collective-permute-done.2
  79.4 1.6 %fusion.1 = f32[256,512]{1,0:T(8,128)} fusion(f32[256,512]{1,0:T(8,128)S(1)} %collective-permute-done.2, f32[256,512]{1,0:T(8,128)S(1)} %copy.25, f32[256,1024]{1,0:T(8,128)S(1)} %constant_dynamic-update-slice_fusion, pred[]{:T(512)} %compare_reduce_fusion), kind=kLoop, calls=%fused_computation.5 | loop fusion | flops 393216 | bytes 2097153 | tf_op jit(solution)/shard_map/add | solution.py:63
  81.0 0.0 reduce-scatter.2.cloned.1.call-update
  81.0 22.0 %reduce-scatter.2.cloned.1.call-done = f32[256,128]{1,0:T(8,128)} async-done(((f32[256,512]{1,0:T(8,128)}), f32[256,128]{1,0:T(8,128)}) %reduce-scatter.2.cloned.1.call-update) | async-done | bytes 131088 | tf_op jit(solution)/shard_map/reduce_scatter | solution.py:64
  (2 shorter events, 0.0 us)
Async XLA Ops:
  6.5 33.1 %all-gather.5.cloned.1.call-start = ((), (), s32[]{:S(2)}) async-start(), calls=%async_computation.1 | async-start | bytes 1310720 | tf_op jit(solution)/shard_map/all_gather | solution.py:29
  8.4 65.4 %all-gather.7.cloned.1.call-start = ((), (), s32[]{:S(2)}) async-start(), calls=%async_computation.3 | async-start | bytes 1310720 | tf_op jit(solution)/shard_map/all_gather | solution.py:8
  39.6 4.8 %collective-permute-start = (bf16[1024,512]{0,1:T(8,128)(2,1)}, bf16[1024,512]{0,1:T(8,128)(2,1)S(1)}, u32[]{:S(2)}, u32[]{:S(2)}) collective-permute-start(bf16[1024,512]{0,1:T(8,128)(2,1)} %all-gather.5.cloned.1.call-done), channel_id=1, source_target_pairs={{16,0},{17,1},{18,2},{19,3},{20,4},{21,5},{22,6},{23,7},{24,8},{25... | collective-permute-start | bytes 3145736 | tf_op jit(solution)/shard_map/ppermute | solution.py:16
  40.9 5.7 %copy-start = (bf16[1024,512]{0,1:T(8,128)(2,1)S(1)}, bf16[1024,512]{0,1:T(8,128)(2,1)}, u32[]{:S(2)}) copy-start(bf16[1024,512]{0,1:T(8,128)(2,1)} %all-gather.5.cloned.1.call-done) | copy-start | bytes 3145732
  46.6 1.4 %copy-start.1 = (bf16[256,128]{1,0:T(8,128)(2,1)S(1)}, bf16[256,128]{1,0:T(8,128)(2,1)}, u32[]{:S(2)}) copy-start(bf16[256,128]{1,0:T(8,128)(2,1)} %param.6) | copy-start | bytes 196612
  47.1 16.2 %copy-start.2 = (s32[128]{0:T(128)S(1)}, s32[128]{0:T(128)}, u32[]{:S(2)}) copy-start(s32[128]{0:T(128)} %param.7) | copy-start | bytes 1540
  47.9 55.1 %reduce-scatter.2.cloned.1.call-start = ((), (), s32[]{:S(2)}) async-start(), calls=%async_computation.2 | async-start | bytes 655360 | tf_op jit(solution)/shard_map/reduce_scatter | solution.py:64
  62.0 16.2 %collective-permute-start.1 = (bf16[256,512]{0,1:T(8,128)(2,1)S(1)}, bf16[256,512]{0,1:T(8,128)(2,1)S(1)}, u32[]{:S(2)}, u32[]{:S(2)}) collective-permute-start(bf16[256,512]{0,1:T(8,128)(2,1)S(1)} %all_gather.19), channel_id=1, source_target_pairs={{16,0},{17,1},{18,2},{19,3},{20,4},{21,5},{22,6},{23,7},{24,8},{25... | collective-permute-start | bytes 786440 | tf_op jit(solution)/shard_map/ppermute | solution.py:16
  75.9 3.5 %collective-permute-start.2 = (f32[256,512]{1,0:T(8,128)S(1)}, f32[256,512]{1,0:T(8,128)S(1)}, u32[]{:S(2)}, u32[]{:S(2)}) collective-permute-start(f32[256,512]{1,0:T(8,128)S(1)} %slice.29), channel_id=1, source_target_pairs={{0,16},{1,17},{2,18},{3,19},{4,20},{5,21},{6,22},{7,23},{8,24},{9,... | collective-permute-start | bytes 1572872 | tf_op jit(solution)/shard_map/ppermute | solution.py:16
Sparse Core Ops, SparseCore 0:
  8.9 30.6 all-gather.4
  48.1 25.6 all-gather.6
  81.1 21.8 reduce-scatter.1
